TPU v7x, 128 devices: a whole 4x4x4 slice. The times are simulated.
128 devices in a mesh: gx: 8 (over x, core), gy: 16 (over z, y).
Axes of the slice: x: 4, y: 4, z: 4, core: 2. Of those that a mesh axis runs over, the one named last changes fastest.
Arguments:
- parent_fields: float32 [5, 4, 384, 6144], P(None, None, 'gx', 'gy'), may hold values from -6 to 6
- parent_velocity: float32 [2, 4, 384, 6144], P(None, None, 'gx', 'gy'), may hold values from -0.3 to 0.3
- parent_mixing: float32 [4, 384, 6144], P(None, 'gx', 'gy'), may hold values from 0.01 to 0.1
- nest_fields: float32 [5, 4, 384, 6144], P(None, None, 'gx', 'gy'), may hold values from -6 to 6
- nest_velocity: float32 [2, 4, 384, 6144], P(None, None, 'gx', 'gy'), may hold values from -0.3 to 0.3
- nest_mixing: float32 [4, 384, 6144], P(None, 'gx', 'gy'), may hold values from 0.01 to 0.1
- nest_anchor: int32 [2], replicated, may hold values from 1 to 3327, as said below
Outputs:
- parent_result: float32 [5, 4, 384, 6144], P(None, None, 'gx', 'gy')
- nest_result: float32 [5, 4, 384, 6144], P(None, None, 'gx', 'gy')
Inputs may be any that keep to these rules, and one draw needn't show every extreme that they name: `nest_anchor`: the row anchor is 1 to 254; the column anchor is 3073 to 3327, so the nest with a rim of one parent cell lies inside the parent grid.
All inputs are finite; a program needn't handle non-finite values.
Results may differ from a plain program's by a relative error of at most 0.00002.
Values sent between devices are 32-bit elements; how exact they have to be, the bound alone decides.
A program may use at most 192 MiB of HBM per device.

v0:
```python
import jax
import jax.numpy as jnp
from jax import lax
from jax.sharding import PartitionSpec as P

SUBSTEPS = 3
third = 1.0 / 3.0
two_thirds = 2.0 / 3.0
nudge_floor = 0.1
relax_width = 4.0


def shift_pairs(count, step):
    return [(i, i + step) for i in range(count) if 0 <= i + step < count]


def neighbours(cells):
    rows = lax.axis_size("gx")
    cols = lax.axis_size("gy")
    western = lax.ppermute(cells[:, :, -1:, :], "gx", shift_pairs(rows, 1))
    eastern = lax.ppermute(cells[:, :, :1, :], "gx", shift_pairs(rows, -1))
    southern = lax.ppermute(cells[:, :, :, -1:], "gy", shift_pairs(cols, 1))
    northern = lax.ppermute(cells[:, :, :, :1], "gy", shift_pairs(cols, -1))
    return (western, eastern, southern, northern)


def update(values, halo, velocity, mixing):
    west_row, east_row, south_col, north_col = halo
    western = jnp.concatenate([west_row, values[:, :, :-1, :]], axis=2)
    eastern = jnp.concatenate([values[:, :, 1:, :], east_row], axis=2)
    southern = jnp.concatenate([south_col, values[:, :, :, :-1]], axis=3)
    northern = jnp.concatenate([values[:, :, :, 1:], north_col], axis=3)
    along_rows = velocity[0]
    along_columns = velocity[1]
    upwind = (
        jnp.maximum(along_rows, 0.0) * (values - western)
        + jnp.minimum(along_rows, 0.0) * (eastern - values)
        + jnp.maximum(along_columns, 0.0) * (values - southern)
        + jnp.minimum(along_columns, 0.0) * (northern - values)
    )
    return values - upwind + mixing * (eastern + western + northern + southern - 4.0 * values)


def refine_rows(block):
    lower = block[:, :, :-2]
    centre = block[:, :, 1:-1]
    upper = block[:, :, 2:]
    stacked = jnp.stack(
        (third * lower + two_thirds * centre, centre, two_thirds * centre + third * upper), axis=3
    )
    extent = centre.shape
    return stacked.reshape(extent[0], extent[1], 3 * extent[2], extent[3])


def refine_columns(block):
    lower = block[:, :, :, :-2]
    centre = block[:, :, :, 1:-1]
    upper = block[:, :, :, 2:]
    stacked = jnp.stack(
        (third * lower + two_thirds * centre, centre, two_thirds * centre + third * upper), axis=4
    )
    extent = centre.shape
    return stacked.reshape(extent[0], extent[1], extent[2], 3 * extent[3])


def block_mean(state):
    extent = state.shape
    grouped = state.reshape(extent[0], extent[1], extent[2] // 3, 3, extent[3] // 3, 3)
    return jnp.sum(grouped, axis=(3, 5)) / 9.0


def relax_weight(row_global, column_global, total_rows, total_columns):
    row_distance = jnp.minimum(row_global, total_rows - 1 - row_global)
    column_distance = jnp.minimum(column_global, total_columns - 1 - column_global)
    distance = jnp.minimum(row_distance[:, None], column_distance[None, :]).astype(jnp.float32)
    return nudge_floor + (1.0 - nudge_floor) * jnp.exp(-distance / relax_width)


def within(positions, limit):
    return (positions >= 0) & (positions < limit)


def column_pairs(count, base, ratio, k, extra):
    pairs = []
    for m in range(count):
        j = ratio * m + k
        p = base + m + extra
        if j < count and p < count:
            pairs.append((p, j))
    return pairs


def per_device(
    parent_fields,
    parent_velocity,
    parent_mixing,
    nest_fields,
    nest_velocity,
    nest_mixing,
    nest_anchor,
):
    row_rank = lax.axis_index("gx")
    column_rank = lax.axis_index("gy")
    row_devices = lax.axis_size("gx")
    column_devices = lax.axis_size("gy")
    parent_rows = parent_fields.shape[2]
    parent_columns = parent_fields.shape[3]
    nest_rows = nest_fields.shape[2]
    nest_columns = nest_fields.shape[3]
    span_rows = nest_rows // 3
    span_columns = nest_columns // 3
    ratio = parent_columns // span_columns
    base = column_devices // 2
    base_column = base * parent_columns
    relay_rows = span_rows + 2
    relay_columns = span_columns + 2
    row_anchor = nest_anchor[0]
    column_anchor = nest_anchor[1]
    offset = column_anchor - 1 - base_column
    parent_next = update(parent_fields, neighbours(parent_fields), parent_velocity, parent_mixing)
    margin = parent_columns - span_columns
    wide = jnp.pad(parent_next, ((0, 0), (0, 0), (0, 0), (margin, margin)))
    relay_cols = None
    for k in range(ratio):
        for extra in (0, 1):
            if extra == 1 and k == 0:
                continue
            start = margin + span_columns * k + offset - extra * parent_columns
            piece = lax.dynamic_slice_in_dim(wide, start, relay_columns, axis=3)
            moved = lax.ppermute(piece, "gy", column_pairs(column_devices, base, ratio, k, extra))
            relay_cols = moved if relay_cols is None else relay_cols + moved
    padded = jnp.pad(relay_cols, ((0, 0), (0, 0), (relay_rows, relay_rows), (0, 0)))
    slots = []
    for target in range(row_devices):
        first = row_anchor - 1 + span_rows * target - parent_rows * row_rank
        first = jnp.clip(first, -relay_rows, parent_rows) + relay_rows
        slots.append(lax.dynamic_slice_in_dim(padded, first, relay_rows, axis=2))
    stacked = jnp.stack(slots, axis=0)
    relay = lax.psum_scatter(stacked, "gx", scatter_dimension=0, tiled=True)[0]
    forcing = refine_columns(refine_rows(relay))
    row_global = row_rank * nest_rows + jnp.arange(nest_rows, dtype=jnp.int32)
    column_global = column_rank * nest_columns + jnp.arange(nest_columns, dtype=jnp.int32)
    weight = relax_weight(
        row_global, column_global, row_devices * nest_rows, column_devices * nest_columns
    )
    state = nest_fields
    for substep in range(SUBSTEPS):
        moved = update(state, neighbours(state), nest_velocity, nest_mixing)
        state = moved + weight * (forcing - moved)
    coarse = block_mean(state)
    gathered = lax.all_gather(coarse, "gx", axis=2, tiled=True)
    total_span = row_devices * span_rows
    gathered = jnp.pad(gathered, ((0, 0), (0, 0), (parent_rows, parent_rows), (0, 0)))
    first = jnp.clip(parent_rows * row_rank - row_anchor, -parent_rows, total_span)
    strip = lax.dynamic_slice_in_dim(gathered, first + parent_rows, parent_rows, axis=2)
    pieces = []
    for extra in (1, 0):
        for k in range(ratio):
            if extra == 1 and k == 0:
                continue
            pairs = [(j, p) for p, j in column_pairs(column_devices, base, ratio, k, extra)]
            pieces.append(lax.ppermute(strip, "gy", pairs))
    joined = jnp.concatenate(pieces, axis=3)
    start = (ratio - 1) * span_columns - 1 - offset
    fed_back = lax.dynamic_slice_in_dim(joined, start, parent_columns, axis=3)
    relative_rows = row_rank * parent_rows + jnp.arange(parent_rows, dtype=jnp.int32) - row_anchor
    relative_columns = (
        column_rank * parent_columns + jnp.arange(parent_columns, dtype=jnp.int32) - column_anchor
    )
    rows_valid = within(relative_rows, total_span)
    columns_valid = within(relative_columns, column_devices * span_columns)
    covered = rows_valid[:, None] & columns_valid[None, :]
    parent_result = jnp.where(covered, fed_back, parent_next)
    return (parent_result, state)


def solution(mesh):
    placed = (
        P(None, None, "gx", "gy"),
        P(None, None, "gx", "gy"),
        P(None, "gx", "gy"),
        P(None, None, "gx", "gy"),
        P(None, None, "gx", "gy"),
        P(None, "gx", "gy"),
        P(),
    )
    return jax.shard_map(
        per_device,
        mesh=mesh,
        in_specs=placed,
        out_specs=(P(None, None, "gx", "gy"), P(None, None, "gx", "gy")),
        check_vma=False,
    )
```

profile of v0, /device:TPU:73, one launch (start us, length us, event | category | flops | bytes accessed | tf_op | source)
XLA Modules:
  0.0 439.8 jit_solution(16195591423806882408)
XLA Ops:
  7.2 2.4 fusion.26
  9.6 3.2 collective-permute-start.6
  12.8 2.1 collective-permute-start.7
  15.6 4.2 collective-permute-start.4
  24.1 2.1 fusion.27
  45.4 4.0 multiply_add_fusion.3
  50.8 2.1 collective-permute-start.10
  61.8 11.4 %collective-permute-done.10 = f32[5,4,48,130]{3,2,1,0:T(8,128)S(1)} collective-permute-done((f32[5,4,48,130]{3,2,1,0:T(8,128)S(1)}, f32[5,4,48,130]{3,2,1,0:T(8,128)S(1)}, u32[]{:S(2)}, u32[]{:S(2)}) %collective-permute-start.10) | collective-permute-done | bytes 499232 | tf_op jit(solution)/shard_map/ppermute | solution.py:130
  73.2 8.7 %collective-permute-start.2 = (f32[5,4,48,1]{3,2,1,0:T(8,128)}, f32[5,4,48,1]{3,2,1,0:T(8,128)}, u32[]{:S(2)}, u32[]{:S(2)}) collective-permute-start(f32[5,4,48,1]{3,2,1,0:T(8,128)} %get-tuple-element.30), channel_id=1, source_target_pairs={{0,1},{1,2},{2,3},{3,4},{4,5},{5,6},{6,7},{7,8},{8,9},{9,10},{10,1... | collective-permute-start | bytes 11528 | tf_op jit(solution)/shard_map/ppermute | solution.py:22
  81.9 20.6 %collective-permute-start.3 = (f32[5,4,48,1]{3,2,1,0:T(8,128)}, f32[5,4,48,1]{3,2,1,0:T(8,128)}, u32[]{:S(2)}, u32[]{:S(2)}) collective-permute-start(f32[5,4,48,1]{3,2,1,0:T(8,128)} %get-tuple-element.31), channel_id=1, source_target_pairs={{1,0},{2,1},{3,2},{4,3},{5,4},{6,5},{7,6},{8,7},{9,8},{10,9},{11,1... | collective-permute-start | bytes 11528 | tf_op jit(solution)/shard_map/ppermute | solution.py:23
  102.6 5.0 %collective-permute-start = (f32[5,4,1,384]{3,1,2,0:T(4,128)}, f32[5,4,1,384]{3,1,2,0:T(4,128)}, u32[]{:S(2)}, u32[]{:S(2)}) collective-permute-start(f32[5,4,1,384]{3,1,2,0:T(4,128)} %copy.336), channel_id=1, source_target_pairs={{0,16},{16,32},{32,48},{48,64},{64,80},{80,96},{96,112},{1,17},{17... | collective-permute-start | bytes 92168 | tf_op jit(solution)/shard_map/ppermute | solution.py:20
  107.6 1.9 collective-permute-start.1
  118.3 2.1 fusion.23
  124.5 81.9 %all-reduce.6.cloned.1.call-done = f32[8,5,4,18,130]{4,2,3,1,0:T(4,128)} async-done(((f32[8,5,4,18,130]{4,2,3,1,0:T(4,128)}), f32[8,5,4,18,130]{4,2,3,1,0:T(4,128)}) %all-reduce.6.cloned.1.call-update) | async-done | bytes 1497616
  209.7 3.6 copy.317
  213.3 3.4 copy.318
  216.8 4.1 multiply_add_fusion.2
  221.4 3.1 collective-permute-start.15
  224.5 2.2 collective-permute-start.16
  226.7 3.6 collective-permute-start.13
  230.4 2.8 collective-permute-start.14
  233.8 2.2 collective-permute-done.14
  238.7 2.9 collective-permute-start.19
  241.5 3.1 collective-permute-start.20
  244.6 5.0 %collective-permute-start.17 = (f32[5,4,1,384]{3,1,2,0:T(4,128)S(1)}, f32[5,4,1,384]{3,1,2,0:T(4,128)S(1)}, u32[]{:S(2)}, u32[]{:S(2)}) collective-permute-start(f32[5,4,1,384]{3,1,2,0:T(4,128)S(1)} %copy.324), channel_id=1, source_target_pairs={{0,16},{16,32},{32,48},{48,64},{64,80},{80,96},{96,112},{1,17},{17... | collective-permute-start | bytes 92168 | tf_op jit(solution)/shard_map/ppermute | solution.py:20
  252.2 3.0 collective-permute-done.18
  257.1 60.9 %reshape.74 = f32[5,4,16,3,128,3]{5,4,3,2,1,0:T(8,128)} reshape(f32[5,4,48,384]{3,2,1,0:T(8,128)S(1)} %multiply_add_fusion) | data formatting | bytes 2949120 | tf_op jit(solution)/shard_map/reshape | solution.py:68
  318.0 20.5 %reduce_sum.9 = f32[5,4,16,128]{3,2,1,0:T(8,128)S(1)} reduce(f32[5,4,16,3,128,3]{5,4,3,2,1,0:T(8,128)} %reshape.74, f32[]{:T(128)} %constant.93.clone.1), dimensions={3,5}, to_apply=%region_1.2 | reduce | flops 327680 | bytes 1638404 | tf_op jit(solution)/shard_map/reduce_sum | solution.py:69
  339.9 32.5 %all-gather.2.cloned.1.call-done = f32[5,4,128,128]{3,1,0,2:T(4,128)} async-done(((f32[5,4,16,128]{3,1,0,2:T(4,128)}), f32[5,4,128,128]{3,1,0,2:T(4,128)}) %all-gather.2.cloned.1.call-update) | async-done | bytes 1310736 | tf_op jit(solution)/shard_map/all_gather | solution.py:151
  375.9 5.3 %collective-permute-start.23 = (f32[5,4,48,128]{3,2,1,0:T(8,128)S(1)}, f32[5,4,48,128]{3,2,1,0:T(8,128)S(1)}, u32[]{:S(2)}, u32[]{:S(2)}) collective-permute-start(f32[5,4,48,128]{3,2,1,0:T(8,128)S(1)} %copy.330), channel_id=1, source_target_pairs={{0,8},{3,9},{6,10},{9,11},{12,12},{15,13},{16,24},{19,25},{22,26},... | collective-permute-start | bytes 1474568 | tf_op jit(solution)/shard_map/ppermute | solution.py:162
  384.5 35.7 %collective-permute-done.21 = f32[5,4,48,128]{3,2,1,0:T(8,128)S(1)} collective-permute-done((f32[5,4,48,128]{3,2,1,0:T(8,128)S(1)}, f32[5,4,48,128]{3,2,1,0:T(8,128)S(1)}, u32[]{:S(2)}, u32[]{:S(2)}) %collective-permute-start.21) | collective-permute-done | bytes 491552 | tf_op jit(solution)/shard_map/ppermute | solution.py:162
  420.4 10.8 %collective-permute-done.25 = f32[5,4,48,128]{3,2,1,0:T(8,128)S(1)} collective-permute-done((f32[5,4,48,128]{3,2,1,0:T(8,128)S(1)}, f32[5,4,48,128]{3,2,1,0:T(8,128)S(1)}, u32[]{:S(2)}, u32[]{:S(2)}) %collective-permute-start.25) | collective-permute-done | bytes 491552 | tf_op jit(solution)/shard_map/ppermute | solution.py:162
  (129 shorter events, 56.0 us)
Async XLA Ops:
  7.2 7.7 %copy-start = (f32[5,4,48,384]{3,2,1,0:T(8,128)S(1)}, f32[5,4,48,384]{3,2,1,0:T(8,128)}, u32[]{:S(2)}) copy-start(f32[5,4,48,384]{3,2,1,0:T(8,128)} %param.7) | copy-start | bytes 4423684
  7.2 199.3 %all-reduce.6.cloned.1.call-start = ((), (), s32[]{:S(2)}) async-start(), calls=%async_computation.1 | async-start | bytes 5898240
  9.6 35.7 %collective-permute-start.6 = (f32[5,4,48,1]{3,2,1,0:T(8,128)}, f32[5,4,48,1]{3,2,1,0:T(8,128)}, u32[]{:S(2)}, u32[]{:S(2)}) collective-permute-start(f32[5,4,48,1]{3,2,1,0:T(8,128)} %get-tuple-element.43), channel_id=1, source_target_pairs={{0,1},{1,2},{2,3},{3,4},{4,5},{5,6},{6,7},{7,8},{8,9},{9,10},{10,1... | collective-permute-start | bytes 11528 | tf_op jit(solution)/shard_map/ppermute | solution.py:22
  12.8 32.5 %collective-permute-start.7 = (f32[5,4,48,1]{3,2,1,0:T(8,128)}, f32[5,4,48,1]{3,2,1,0:T(8,128)}, u32[]{:S(2)}, u32[]{:S(2)}) collective-permute-start(f32[5,4,48,1]{3,2,1,0:T(8,128)} %get-tuple-element.44), channel_id=1, source_target_pairs={{1,0},{2,1},{3,2},{4,3},{5,4},{6,5},{7,6},{8,7},{9,8},{10,9},{11,1... | collective-permute-start | bytes 11528 | tf_op jit(solution)/shard_map/ppermute | solution.py:23
  15.6 28.2 %collective-permute-start.4 = (f32[5,4,1,384]{3,1,2,0:T(4,128)}, f32[5,4,1,384]{3,1,2,0:T(4,128)}, u32[]{:S(2)}, u32[]{:S(2)}) collective-permute-start(f32[5,4,1,384]{3,1,2,0:T(4,128)} %copy.338), channel_id=1, source_target_pairs={{0,16},{16,32},{32,48},{48,64},{64,80},{80,96},{96,112},{1,17},{17... | collective-permute-start | bytes 92168 | tf_op jit(solution)/shard_map/ppermute | solution.py:20
  20.4 24.1 %collective-permute-start.5 = (f32[5,4,1,384]{3,1,2,0:T(4,128)}, f32[5,4,1,384]{3,1,2,0:T(4,128)}, u32[]{:S(2)}, u32[]{:S(2)}) collective-permute-start(f32[5,4,1,384]{3,1,2,0:T(4,128)} %copy.339), channel_id=1, source_target_pairs={{16,0},{32,16},{48,32},{64,48},{80,64},{96,80},{112,96},{17,1},{33... | collective-permute-start | bytes 92168 | tf_op jit(solution)/shard_map/ppermute | solution.py:21
  49.4 9.6 %copy-start.10 = (f32[2,4,48,384]{3,2,1,0:T(8,128)S(1)}, f32[2,4,48,384]{3,2,1,0:T(8,128)}, u32[]{:S(2)}) copy-start(f32[2,4,48,384]{3,2,1,0:T(8,128)} %param.11) | copy-start | bytes 1769476
  50.8 22.4 %collective-permute-start.10 = (f32[5,4,48,130]{3,2,1,0:T(8,128)S(1)}, f32[5,4,48,130]{3,2,1,0:T(8,128)S(1)}, u32[]{:S(2)}, u32[]{:S(2)}) collective-permute-start(f32[5,4,48,130]{3,2,1,0:T(8,128)S(1)} %get-tuple-element.35), channel_id=1, source_target_pairs={{9,1},{10,4},{11,7},{12,10},{13,13},{25,17},{26,20},{27,23},{28,26... | collective-permute-start | bytes 1497608 | tf_op jit(solution)/shard_map/ppermute | solution.py:130
  53.0 29.0 %collective-permute-start.11 = (f32[5,4,48,130]{3,2,1,0:T(8,128)S(1)}, f32[5,4,48,130]{3,2,1,0:T(8,128)S(1)}, u32[]{:S(2)}, u32[]{:S(2)}) collective-permute-start(f32[5,4,48,130]{3,2,1,0:T(8,128)S(1)} %get-tuple-element.36), channel_id=1, source_target_pairs={{8,2},{9,5},{10,8},{11,11},{12,14},{24,18},{25,21},{26,24},{27,27}... | collective-permute-start | bytes 1497608 | tf_op jit(solution)/shard_map/ppermute | solution.py:130
  54.3 48.2 %collective-permute-start.12 = (f32[5,4,48,130]{3,2,1,0:T(8,128)S(1)}, f32[5,4,48,130]{3,2,1,0:T(8,128)S(1)}, u32[]{:S(2)}, u32[]{:S(2)}) collective-permute-start(f32[5,4,48,130]{3,2,1,0:T(8,128)S(1)} %get-tuple-element.37), channel_id=1, source_target_pairs={{9,2},{10,5},{11,8},{12,11},{13,14},{25,18},{26,21},{27,24},{28,27... | collective-permute-start | bytes 1497608 | tf_op jit(solution)/shard_map/ppermute | solution.py:130
  55.7 51.9 %collective-permute-start.8 = (f32[5,4,48,130]{3,2,1,0:T(8,128)S(1)}, f32[5,4,48,130]{3,2,1,0:T(8,128)S(1)}, u32[]{:S(2)}, u32[]{:S(2)}) collective-permute-start(f32[5,4,48,130]{3,2,1,0:T(8,128)S(1)} %get-tuple-element.38), channel_id=1, source_target_pairs={{8,0},{9,3},{10,6},{11,9},{12,12},{13,15},{24,16},{25,19},{26,22},... | collective-permute-start | bytes 1497608 | tf_op jit(solution)/shard_map/ppermute | solution.py:130
  57.6 52.0 %collective-permute-start.9 = (f32[5,4,48,130]{3,2,1,0:T(8,128)S(1)}, f32[5,4,48,130]{3,2,1,0:T(8,128)S(1)}, u32[]{:S(2)}, u32[]{:S(2)}) collective-permute-start(f32[5,4,48,130]{3,2,1,0:T(8,128)S(1)} %get-tuple-element.34), channel_id=1, source_target_pairs={{8,1},{9,4},{10,7},{11,10},{12,13},{24,17},{25,20},{26,23},{27,26}... | collective-permute-start | bytes 1497608 | tf_op jit(solution)/shard_map/ppermute | solution.py:130
  73.2 143.6 %collective-permute-start.2 = (f32[5,4,48,1]{3,2,1,0:T(8,128)}, f32[5,4,48,1]{3,2,1,0:T(8,128)}, u32[]{:S(2)}, u32[]{:S(2)}) collective-permute-start(f32[5,4,48,1]{3,2,1,0:T(8,128)} %get-tuple-element.30), channel_id=1, source_target_pairs={{0,1},{1,2},{2,3},{3,4},{4,5},{5,6},{6,7},{7,8},{8,9},{9,10},{10,1... | collective-permute-start | bytes 11528 | tf_op jit(solution)/shard_map/ppermute | solution.py:22
  81.9 134.8 %collective-permute-start.3 = (f32[5,4,48,1]{3,2,1,0:T(8,128)}, f32[5,4,48,1]{3,2,1,0:T(8,128)}, u32[]{:S(2)}, u32[]{:S(2)}) collective-permute-start(f32[5,4,48,1]{3,2,1,0:T(8,128)} %get-tuple-element.31), channel_id=1, source_target_pairs={{1,0},{2,1},{3,2},{4,3},{5,4},{6,5},{7,6},{8,7},{9,8},{10,9},{11,1... | collective-permute-start | bytes 11528 | tf_op jit(solution)/shard_map/ppermute | solution.py:23
  102.6 19.2 %collective-permute-start = (f32[5,4,1,384]{3,1,2,0:T(4,128)}, f32[5,4,1,384]{3,1,2,0:T(4,128)}, u32[]{:S(2)}, u32[]{:S(2)}) collective-permute-start(f32[5,4,1,384]{3,1,2,0:T(4,128)} %copy.336), channel_id=1, source_target_pairs={{0,16},{16,32},{32,48},{48,64},{64,80},{80,96},{96,112},{1,17},{17... | collective-permute-start | bytes 92168 | tf_op jit(solution)/shard_map/ppermute | solution.py:20
  107.6 15.5 %collective-permute-start.1 = (f32[5,4,1,384]{3,1,2,0:T(4,128)}, f32[5,4,1,384]{3,1,2,0:T(4,128)}, u32[]{:S(2)}, u32[]{:S(2)}) collective-permute-start(f32[5,4,1,384]{3,1,2,0:T(4,128)} %copy.337), channel_id=1, source_target_pairs={{16,0},{32,16},{48,32},{64,48},{80,64},{96,80},{112,96},{17,1},{33... | collective-permute-start | bytes 92168 | tf_op jit(solution)/shard_map/ppermute | solution.py:21
  118.0 254.4 %all-gather.2.cloned.1.call-start = ((), (), s32[]{:S(2)}) async-start(), calls=%async_computation | async-start | bytes 1474560 | tf_op jit(solution)/shard_map/all_gather | solution.py:151
  221.4 14.6 %collective-permute-start.15 = (f32[5,4,48,1]{3,2,1,0:T(8,128)S(1)}, f32[5,4,48,1]{3,2,1,0:T(8,128)S(1)}, u32[]{:S(2)}, u32[]{:S(2)}) collective-permute-start(f32[5,4,48,1]{3,2,1,0:T(8,128)S(1)} %get-tuple-element.22), channel_id=1, source_target_pairs={{0,1},{1,2},{2,3},{3,4},{4,5},{5,6},{6,7},{7,8},{8,9},{9,10},{10,1... | collective-permute-start | bytes 11528 | tf_op jit(solution)/shard_map/ppermute | solution.py:22
  224.5 11.8 %collective-permute-start.16 = (f32[5,4,48,1]{3,2,1,0:T(8,128)S(1)}, f32[5,4,48,1]{3,2,1,0:T(8,128)S(1)}, u32[]{:S(2)}, u32[]{:S(2)}) collective-permute-start(f32[5,4,48,1]{3,2,1,0:T(8,128)S(1)} %get-tuple-element.23), channel_id=1, source_target_pairs={{1,0},{2,1},{3,2},{4,3},{5,4},{6,5},{7,6},{8,7},{9,8},{10,9},{11,1... | collective-permute-start | bytes 11528 | tf_op jit(solution)/shard_map/ppermute | solution.py:23
  226.7 7.0 %collective-permute-start.13 = (f32[5,4,1,384]{3,1,2,0:T(4,128)S(1)}, f32[5,4,1,384]{3,1,2,0:T(4,128)S(1)}, u32[]{:S(2)}, u32[]{:S(2)}) collective-permute-start(f32[5,4,1,384]{3,1,2,0:T(4,128)S(1)} %copy.319), channel_id=1, source_target_pairs={{0,16},{16,32},{32,48},{48,64},{64,80},{80,96},{96,112},{1,17},{17... | collective-permute-start | bytes 92168 | tf_op jit(solution)/shard_map/ppermute | solution.py:20
  230.4 5.6 %collective-permute-start.14 = (f32[5,4,1,384]{3,1,2,0:T(4,128)S(1)}, f32[5,4,1,384]{3,1,2,0:T(4,128)S(1)}, u32[]{:S(2)}, u32[]{:S(2)}) collective-permute-start(f32[5,4,1,384]{3,1,2,0:T(4,128)S(1)} %copy.321), channel_id=1, source_target_pairs={{16,0},{32,16},{48,32},{64,48},{80,64},{96,80},{112,96},{17,1},{33... | collective-permute-start | bytes 92168 | tf_op jit(solution)/shard_map/ppermute | solution.py:21
  238.7 16.6 %collective-permute-start.19 = (f32[5,4,48,1]{3,2,1,0:T(8,128)S(1)}, f32[5,4,48,1]{3,2,1,0:T(8,128)S(1)}, u32[]{:S(2)}, u32[]{:S(2)}) collective-permute-start(f32[5,4,48,1]{3,2,1,0:T(8,128)S(1)} %get-tuple-element.14), channel_id=1, source_target_pairs={{0,1},{1,2},{2,3},{3,4},{4,5},{5,6},{6,7},{7,8},{8,9},{9,10},{10,1... | collective-permute-start | bytes 11528 | tf_op jit(solution)/shard_map/ppermute | solution.py:22
  241.5 13.7 %collective-permute-start.20 = (f32[5,4,48,1]{3,2,1,0:T(8,128)S(1)}, f32[5,4,48,1]{3,2,1,0:T(8,128)S(1)}, u32[]{:S(2)}, u32[]{:S(2)}) collective-permute-start(f32[5,4,48,1]{3,2,1,0:T(8,128)S(1)} %get-tuple-element.15), channel_id=1, source_target_pairs={{1,0},{2,1},{3,2},{4,3},{5,4},{6,5},{7,6},{8,7},{9,8},{10,9},{11,1... | collective-permute-start | bytes 11528 | tf_op jit(solution)/shard_map/ppermute | solution.py:23
  244.6 7.5 %collective-permute-start.17 = (f32[5,4,1,384]{3,1,2,0:T(4,128)S(1)}, f32[5,4,1,384]{3,1,2,0:T(4,128)S(1)}, u32[]{:S(2)}, u32[]{:S(2)}) collective-permute-start(f32[5,4,1,384]{3,1,2,0:T(4,128)S(1)} %copy.324), channel_id=1, source_target_pairs={{0,16},{16,32},{32,48},{48,64},{64,80},{80,96},{96,112},{1,17},{17... | collective-permute-start | bytes 92168 | tf_op jit(solution)/shard_map/ppermute | solution.py:20
  249.7 5.5 %collective-permute-start.18 = (f32[5,4,1,384]{3,1,2,0:T(4,128)S(1)}, f32[5,4,1,384]{3,1,2,0:T(4,128)S(1)}, u32[]{:S(2)}, u32[]{:S(2)}) collective-permute-start(f32[5,4,1,384]{3,1,2,0:T(4,128)S(1)} %copy.326), channel_id=1, source_target_pairs={{16,0},{32,16},{48,32},{64,48},{80,64},{96,80},{112,96},{17,1},{33... | collective-permute-start | bytes 92168 | tf_op jit(solution)/shard_map/ppermute | solution.py:21
  257.1 61.0 %copy-start.4 = (f32[5,4,48,384]{3,2,1,0:T(8,128)}, f32[5,4,48,384]{3,2,1,0:T(8,128)S(1)}, u32[]{:S(2)}) copy-start(f32[5,4,48,384]{3,2,1,0:T(8,128)S(1)} %multiply_add_fusion) | copy-start | bytes 4423684
  372.6 47.6 %collective-permute-start.21 = (f32[5,4,48,128]{3,2,1,0:T(8,128)S(1)}, f32[5,4,48,128]{3,2,1,0:T(8,128)S(1)}, u32[]{:S(2)}, u32[]{:S(2)}) collective-permute-start(f32[5,4,48,128]{3,2,1,0:T(8,128)S(1)} %copy.330), channel_id=1, source_target_pairs={{1,9},{4,10},{7,11},{10,12},{13,13},{17,25},{20,26},{23,27},{26,28... | collective-permute-start | bytes 1474568 | tf_op jit(solution)/shard_map/ppermute | solution.py:162
  373.9 46.4 %collective-permute-start.22 = (f32[5,4,48,128]{3,2,1,0:T(8,128)S(1)}, f32[5,4,48,128]{3,2,1,0:T(8,128)S(1)}, u32[]{:S(2)}, u32[]{:S(2)}) collective-permute-start(f32[5,4,48,128]{3,2,1,0:T(8,128)S(1)} %copy.330), channel_id=1, source_target_pairs={{2,9},{5,10},{8,11},{11,12},{14,13},{18,25},{21,26},{24,27},{27,28... | collective-permute-start | bytes 1474568 | tf_op jit(solution)/shard_map/ppermute | solution.py:162
  375.9 44.5 %collective-permute-start.23 = (f32[5,4,48,128]{3,2,1,0:T(8,128)S(1)}, f32[5,4,48,128]{3,2,1,0:T(8,128)S(1)}, u32[]{:S(2)}, u32[]{:S(2)}) collective-permute-start(f32[5,4,48,128]{3,2,1,0:T(8,128)S(1)} %copy.330), channel_id=1, source_target_pairs={{0,8},{3,9},{6,10},{9,11},{12,12},{15,13},{16,24},{19,25},{22,26},... | collective-permute-start | bytes 1474568 | tf_op jit(solution)/shard_map/ppermute | solution.py:162
  381.8 38.6 %collective-permute-start.24 = (f32[5,4,48,128]{3,2,1,0:T(8,128)S(1)}, f32[5,4,48,128]{3,2,1,0:T(8,128)S(1)}, u32[]{:S(2)}, u32[]{:S(2)}) collective-permute-start(f32[5,4,48,128]{3,2,1,0:T(8,128)S(1)} %copy.330), channel_id=1, source_target_pairs={{1,8},{4,9},{7,10},{10,11},{13,12},{17,24},{20,25},{23,26},{26,27}... | collective-permute-start | bytes 1474568 | tf_op jit(solution)/shard_map/ppermute | solution.py:162
  383.2 48.1 %collective-permute-start.25 = (f32[5,4,48,128]{3,2,1,0:T(8,128)S(1)}, f32[5,4,48,128]{3,2,1,0:T(8,128)S(1)}, u32[]{:S(2)}, u32[]{:S(2)}) collective-permute-start(f32[5,4,48,128]{3,2,1,0:T(8,128)S(1)} %copy.330), channel_id=1, source_target_pairs={{2,8},{5,9},{8,10},{11,11},{14,12},{18,24},{21,25},{24,26},{27,27}... | collective-permute-start | bytes 1474568 | tf_op jit(solution)/shard_map/ppermute | solution.py:162
  420.3 11.0 %copy-start.3 = (f32[5,4,48,384]{3,2,1,0:T(8,128)S(1)}, f32[5,4,48,384]{3,2,1,0:T(8,128)}, u32[]{:S(2)}) copy-start(f32[5,4,48,384]{3,2,1,0:T(8,128)} %copy-done.2) | copy-start | bytes 4423684
  (9 other events, 34.7 us)
Sparse Core Ops, SparseCore 0:
  118.2 88.2 all-reduce.5
  339.4 32.9 all-gather.1
where the time goes:
time: 441 us; the launch traced here: 440 us
  waiting for transfers between devices  178 us (40%)
  local copies, waits for them, and re-layouts  104 us (24%)
  starting transfers between devices  91.2 us (21%)
  other arithmetic  39.5 us (9%)
  between operations  27 us (6%)
    unnamed x3, waiting for transfers between devices  81.9 us
    reshape x1, local copies, waits for them, and re-layouts, block_mean(): state.reshape(extent[0], extent[1], extent[2] // 3, 3, extent[3] // 3, 3)  60.9 us
    ppermute x5, waiting for transfers between devices, per_device(): pieces.append(lax.ppermute(strip, 'gy', pairs))  46.6 us
    all_gather x1, waiting for transfers between devices, per_device(): gathered = lax.all_gather(coarse, 'gx', axis=2, tiled=True)  32.5 us
    ppermute x4, starting transfers between devices, neighbours(): northern = lax.ppermute(cells[:, :, :, :1], 'gy', shift_pairs(cols, -1))  28 us
    reduce_sum x1, other arithmetic, block_mean(): return jnp.sum(grouped, axis=(3, 5)) / 9.0  20.5 us
    ppermute x4, starting transfers between devices, neighbours(): southern = lax.ppermute(cells[:, :, :, -1:], 'gy', shift_pairs(cols, 1))  17.9 us
    ppermute x4, starting transfers between devices, neighbours(): western = lax.ppermute(cells[:, :, -1:, :], 'gx', shift_pairs(rows, 1))  17.9 us
  transfers between devices with their start and end apart: 28, of which 8 were waited for; matrix products, arithmetic and copies ran while one was open for 10% of the time, Pallas kernels for 0%

commit v1 on v0

--- a/solution.py
+++ b/solution.py
@@ -8,6 +8,13 @@
 two_thirds = 2.0 / 3.0
 nudge_floor = 0.1
 relax_width = 4.0
+
+
+def exchange_gather(x, axis, d):
+    count = lax.axis_size(axis)
+    blocks = jnp.stack([x for _ in range(count)])
+    blocks = lax.all_to_all(blocks, axis, split_axis=0, concat_axis=0)
+    return jnp.concatenate(blocks, axis=d)
 
 
 def shift_pairs(count, step):
@@ -148,7 +155,7 @@
         moved = update(state, neighbours(state), nest_velocity, nest_mixing)
         state = moved + weight * (forcing - moved)
     coarse = block_mean(state)
-    gathered = lax.all_gather(coarse, "gx", axis=2, tiled=True)
+    gathered = exchange_gather(coarse, "gx", 2)
     total_span = row_devices * span_rows
     gathered = jnp.pad(gathered, ((0, 0), (0, 0), (parent_rows, parent_rows), (0, 0)))
     first = jnp.clip(parent_rows * row_rank - row_anchor, -parent_rows, total_span)

time: 441 us -> 439 us (level)
  waiting for transfers between devices: 178 us -> 164 us
  starting transfers between devices: 91.2 us -> 103 us
    all_gather x1 -> x0, waiting for transfers between devices: 32.5 us -> none  [per_device(): gathered = lax.all_gather(coarse, 'gx', axis=2, tiled=True)]
    all_to_all x0 -> x1, waiting for transfers between devices: none -> 17.3 us  [exchange_gather(): blocks = lax.all_to_all(blocks, axis, split_axis=0, concat_axis=0)]
    all_to_all x0 -> x1, starting transfers between devices: none -> 11 us  [exchange_gather(): blocks = lax.all_to_all(blocks, axis, split_axis=0, concat_axis=0)]
    unnamed x3 -> x2, waiting for transfers between devices: 81.9 us -> 83.5 us
    unnamed x42 -> x44, local copies, waits for them, and re-layouts: 11 us -> 11 us
  transfers between devices with their start and end apart: 28 -> 28, of which waited for: 8 -> 8; matrix products, arithmetic and copies ran while one was open for 10% -> 9% of each run, Pallas kernels for 0% -> 0%
where the time goes in v1:
time: 439 us; the launch traced here: 438 us
  waiting for transfers between devices  164 us (37%)
  local copies, waits for them, and re-layouts  104 us (24%)
  starting transfers between devices  103 us (23%)
  other arithmetic  40.4 us (9%)
  between operations  27 us (6%)
    unnamed x2, waiting for transfers between devices  83.5 us
    reshape x1, local copies, waits for them, and re-layouts, block_mean(): state.reshape(extent[0], extent[1], extent[2] // 3, 3, extent[3] // 3, 3)  61.7 us
    ppermute x5, waiting for transfers between devices, per_device(): pieces.append(lax.ppermute(strip, 'gy', pairs))  46 us
    ppermute x4, starting transfers between devices, neighbours(): northern = lax.ppermute(cells[:, :, :, :1], 'gy', shift_pairs(cols, -1))  28 us
    reduce_sum x1, other arithmetic, block_mean(): return jnp.sum(grouped, axis=(3, 5)) / 9.0  20.5 us
    ppermute x4, starting transfers between devices, neighbours(): southern = lax.ppermute(cells[:, :, :, -1:], 'gy', shift_pairs(cols, 1))  17.9 us
    ppermute x4, starting transfers between devices, neighbours(): western = lax.ppermute(cells[:, :, -1:, :], 'gx', shift_pairs(rows, 1))  17.9 us
    all_to_all x1, waiting for transfers between devices, exchange_gather(): blocks = lax.all_to_all(blocks, axis, split_axis=0, concat_axis=0)  17.3 us
  transfers between devices with their start and end apart: 28, of which 8 were waited for; matrix products, arithmetic and copies ran while one was open for 9% of the time, Pallas kernels for 0%

profile of v1, /device:TPU:73, one launch (start us, length us, event | category | flops | bytes accessed | tf_op | source)
XLA Modules:
  0.0 437.6 jit_solution(17489004870840350718)
XLA Ops:
  7.2 2.4 fusion.26
  9.6 3.2 collective-permute-start.6
  15.6 4.2 collective-permute-start.4
  45.4 4.0 multiply_add_fusion.3
  50.8 2.1 collective-permute-start.10
  61.8 11.4 %collective-permute-done.10 = f32[5,4,48,130]{3,2,1,0:T(8,128)S(1)} collective-permute-done((f32[5,4,48,130]{3,2,1,0:T(8,128)S(1)}, f32[5,4,48,130]{3,2,1,0:T(8,128)S(1)}, u32[]{:S(2)}, u32[]{:S(2)}) %collective-permute-start.10) | collective-permute-done | bytes 499232 | tf_op jit(solution)/shard_map/ppermute | solution.py:137
  73.2 8.7 %collective-permute-start.2 = (f32[5,4,48,1]{3,2,1,0:T(8,128)}, f32[5,4,48,1]{3,2,1,0:T(8,128)}, u32[]{:S(2)}, u32[]{:S(2)}) collective-permute-start(f32[5,4,48,1]{3,2,1,0:T(8,128)} %get-tuple-element.30), channel_id=1, source_target_pairs={{0,1},{1,2},{2,3},{3,4},{4,5},{5,6},{6,7},{7,8},{8,9},{9,10},{10,1... | collective-permute-start | bytes 11528 | tf_op jit(solution)/shard_map/ppermute | solution.py:29
  81.9 20.6 %collective-permute-start.3 = (f32[5,4,48,1]{3,2,1,0:T(8,128)}, f32[5,4,48,1]{3,2,1,0:T(8,128)}, u32[]{:S(2)}, u32[]{:S(2)}) collective-permute-start(f32[5,4,48,1]{3,2,1,0:T(8,128)} %get-tuple-element.31), channel_id=1, source_target_pairs={{1,0},{2,1},{3,2},{4,3},{5,4},{6,5},{7,6},{8,7},{9,8},{10,9},{11,1... | collective-permute-start | bytes 11528 | tf_op jit(solution)/shard_map/ppermute | solution.py:30
  102.6 5.0 %collective-permute-start = (f32[5,4,1,384]{3,1,2,0:T(4,128)S(1)}, f32[5,4,1,384]{3,1,2,0:T(4,128)S(1)}, u32[]{:S(2)}, u32[]{:S(2)}) collective-permute-start(f32[5,4,1,384]{3,1,2,0:T(4,128)S(1)} %copy-done.11), channel_id=1, source_target_pairs={{0,16},{16,32},{32,48},{48,64},{64,80},{80,96},{96,112},{1,17},{17... | collective-permute-start | bytes 92168 | tf_op jit(solution)/shard_map/ppermute | solution.py:27
  107.7 2.1 collective-permute-start.1
  123.0 83.5 %all-reduce.6.cloned.1.call-done = f32[8,5,4,18,130]{4,2,3,1,0:T(4,128)} async-done(((f32[8,5,4,18,130]{4,2,3,1,0:T(4,128)}), f32[8,5,4,18,130]{4,2,3,1,0:T(4,128)}) %all-reduce.6.cloned.1.call-update) | async-done | bytes 1497616
  209.7 3.6 copy.308
  213.3 3.4 copy.309
  216.7 4.1 multiply_add_fusion.2
  221.3 3.1 collective-permute-start.15
  224.5 2.2 collective-permute-start.16
  226.7 3.6 collective-permute-start.13
  230.3 2.8 collective-permute-start.14
  233.7 2.2 collective-permute-done.14
  238.6 2.9 collective-permute-start.19
  241.5 3.1 collective-permute-start.20
  244.6 5.0 %collective-permute-start.17 = (f32[5,4,1,384]{3,1,2,0:T(4,128)S(1)}, f32[5,4,1,384]{3,1,2,0:T(4,128)S(1)}, u32[]{:S(2)}, u32[]{:S(2)}) collective-permute-start(f32[5,4,1,384]{3,1,2,0:T(4,128)S(1)} %copy.315), channel_id=1, source_target_pairs={{0,16},{16,32},{32,48},{48,64},{64,80},{80,96},{96,112},{1,17},{17... | collective-permute-start | bytes 92168 | tf_op jit(solution)/shard_map/ppermute | solution.py:27
  249.6 2.1 collective-permute-start.18
  252.3 2.8 collective-permute-done.18
  255.2 2.6 multiply_add_fusion
  257.8 61.7 %reshape.82 = f32[5,4,16,3,128,3]{5,4,3,2,1,0:T(8,128)} reshape(f32[5,4,48,384]{3,2,1,0:T(8,128)} %multiply_add_fusion) | data formatting | bytes 2949120 | tf_op jit(solution)/shard_map/reshape | solution.py:75
  319.5 20.5 %reduce_sum.9 = f32[5,4,16,128]{3,2,1,0:T(8,128)S(1)} reduce(f32[5,4,16,3,128,3]{5,4,3,2,1,0:T(8,128)} %reshape.82, f32[]{:T(128)} %constant.93.clone.1), dimensions={3,5}, to_apply=%region_1.2 | reduce | flops 327680 | bytes 1638404 | tf_op jit(solution)/shard_map/reduce_sum | solution.py:76
  341.3 11.0 %all-to-all-start = ((f32[8,5,4,16,128]{4,3,2,1,0:T(8,128)}), f32[8,5,4,16,128]{4,3,2,1,0:T(8,128)S(1)}, u32[]{:S(2)}, u32[]{:S(2)}) async-start(f32[8,5,4,16,128]{4,3,2,1,0:T(8,128)} %stack.79), calls=%async_computation | async-start | bytes 2621440 | tf_op jit(solution)/shard_map/all_to_all | solution.py:16
  352.9 17.3 %all-to-all-done = f32[8,5,4,16,128]{4,3,2,1,0:T(8,128)S(1)} async-done(((f32[8,5,4,16,128]{4,3,2,1,0:T(8,128)}), f32[8,5,4,16,128]{4,3,2,1,0:T(8,128)S(1)}, u32[]{:S(2)}, u32[]{:S(2)}) %all-to-all-start) | async-done | bytes 1310752 | tf_op jit(solution)/shard_map/all_to_all | solution.py:16
  373.7 5.8 %collective-permute-start.23 = (f32[5,4,48,128]{3,2,1,0:T(8,128)S(1)}, f32[5,4,48,128]{3,2,1,0:T(8,128)S(1)}, u32[]{:S(2)}, u32[]{:S(2)}) collective-permute-start(f32[5,4,48,128]{3,2,1,0:T(8,128)S(1)} %pad_dynamic-slice_fusion.13), channel_id=1, source_target_pairs={{0,8},{3,9},{6,10},{9,11},{12,12},{15,13},{16,24},{19,25},{22,26},... | collective-permute-start | bytes 1474568 | tf_op jit(solution)/shard_map/ppermute | solution.py:169
  382.9 34.5 %collective-permute-done.21 = f32[5,4,48,128]{3,2,1,0:T(8,128)S(1)} collective-permute-done((f32[5,4,48,128]{3,2,1,0:T(8,128)S(1)}, f32[5,4,48,128]{3,2,1,0:T(8,128)S(1)}, u32[]{:S(2)}, u32[]{:S(2)}) %collective-permute-start.21) | collective-permute-done | bytes 491552 | tf_op jit(solution)/shard_map/ppermute | solution.py:169
  417.5 11.6 %collective-permute-done.25 = f32[5,4,48,128]{3,2,1,0:T(8,128)S(1)} collective-permute-done((f32[5,4,48,128]{3,2,1,0:T(8,128)S(1)}, f32[5,4,48,128]{3,2,1,0:T(8,128)S(1)}, u32[]{:S(2)}, u32[]{:S(2)}) %collective-permute-start.25) | collective-permute-done | bytes 491552 | tf_op jit(solution)/shard_map/ppermute | solution.py:169
  (130 shorter events, 57.3 us)
Async XLA Ops:
  7.2 199.3 %all-reduce.6.cloned.1.call-start = ((), (), s32[]{:S(2)}) async-start(), calls=%async_computation.1 | async-start | bytes 5898240
  9.6 35.7 %collective-permute-start.6 = (f32[5,4,48,1]{3,2,1,0:T(8,128)}, f32[5,4,48,1]{3,2,1,0:T(8,128)}, u32[]{:S(2)}, u32[]{:S(2)}) collective-permute-start(f32[5,4,48,1]{3,2,1,0:T(8,128)} %get-tuple-element.43), channel_id=1, source_target_pairs={{0,1},{1,2},{2,3},{3,4},{4,5},{5,6},{6,7},{7,8},{8,9},{9,10},{10,1... | collective-permute-start | bytes 11528 | tf_op jit(solution)/shard_map/ppermute | solution.py:29
  12.8 32.6 %collective-permute-start.7 = (f32[5,4,48,1]{3,2,1,0:T(8,128)}, f32[5,4,48,1]{3,2,1,0:T(8,128)}, u32[]{:S(2)}, u32[]{:S(2)}) collective-permute-start(f32[5,4,48,1]{3,2,1,0:T(8,128)} %get-tuple-element.44), channel_id=1, source_target_pairs={{1,0},{2,1},{3,2},{4,3},{5,4},{6,5},{7,6},{8,7},{9,8},{10,9},{11,1... | collective-permute-start | bytes 11528 | tf_op jit(solution)/shard_map/ppermute | solution.py:30
  15.6 28.2 %collective-permute-start.4 = (f32[5,4,1,384]{3,1,2,0:T(4,128)}, f32[5,4,1,384]{3,1,2,0:T(4,128)}, u32[]{:S(2)}, u32[]{:S(2)}) collective-permute-start(f32[5,4,1,384]{3,1,2,0:T(4,128)} %copy.324), channel_id=1, source_target_pairs={{0,16},{16,32},{32,48},{48,64},{64,80},{80,96},{96,112},{1,17},{17... | collective-permute-start | bytes 92168 | tf_op jit(solution)/shard_map/ppermute | solution.py:27
  20.4 24.1 %collective-permute-start.5 = (f32[5,4,1,384]{3,1,2,0:T(4,128)}, f32[5,4,1,384]{3,1,2,0:T(4,128)}, u32[]{:S(2)}, u32[]{:S(2)}) collective-permute-start(f32[5,4,1,384]{3,1,2,0:T(4,128)} %copy.325), channel_id=1, source_target_pairs={{16,0},{32,16},{48,32},{64,48},{80,64},{96,80},{112,96},{17,1},{33... | collective-permute-start | bytes 92168 | tf_op jit(solution)/shard_map/ppermute | solution.py:28
  49.4 9.6 %copy-start.9 = (f32[2,4,48,384]{3,2,1,0:T(8,128)S(1)}, f32[2,4,48,384]{3,2,1,0:T(8,128)}, u32[]{:S(2)}) copy-start(f32[2,4,48,384]{3,2,1,0:T(8,128)} %param.11) | copy-start | bytes 1769476
  50.8 22.4 %collective-permute-start.10 = (f32[5,4,48,130]{3,2,1,0:T(8,128)S(1)}, f32[5,4,48,130]{3,2,1,0:T(8,128)S(1)}, u32[]{:S(2)}, u32[]{:S(2)}) collective-permute-start(f32[5,4,48,130]{3,2,1,0:T(8,128)S(1)} %get-tuple-element.35), channel_id=1, source_target_pairs={{9,1},{10,4},{11,7},{12,10},{13,13},{25,17},{26,20},{27,23},{28,26... | collective-permute-start | bytes 1497608 | tf_op jit(solution)/shard_map/ppermute | solution.py:137
  53.0 29.0 %collective-permute-start.11 = (f32[5,4,48,130]{3,2,1,0:T(8,128)S(1)}, f32[5,4,48,130]{3,2,1,0:T(8,128)S(1)}, u32[]{:S(2)}, u32[]{:S(2)}) collective-permute-start(f32[5,4,48,130]{3,2,1,0:T(8,128)S(1)} %get-tuple-element.36), channel_id=1, source_target_pairs={{8,2},{9,5},{10,8},{11,11},{12,14},{24,18},{25,21},{26,24},{27,27}... | collective-permute-start | bytes 1497608 | tf_op jit(solution)/shard_map/ppermute | solution.py:137
  54.3 48.2 %collective-permute-start.12 = (f32[5,4,48,130]{3,2,1,0:T(8,128)S(1)}, f32[5,4,48,130]{3,2,1,0:T(8,128)S(1)}, u32[]{:S(2)}, u32[]{:S(2)}) collective-permute-start(f32[5,4,48,130]{3,2,1,0:T(8,128)S(1)} %get-tuple-element.37), channel_id=1, source_target_pairs={{9,2},{10,5},{11,8},{12,11},{13,14},{25,18},{26,21},{27,24},{28,27... | collective-permute-start | bytes 1497608 | tf_op jit(solution)/shard_map/ppermute | solution.py:137
  55.7 52.0 %collective-permute-start.8 = (f32[5,4,48,130]{3,2,1,0:T(8,128)S(1)}, f32[5,4,48,130]{3,2,1,0:T(8,128)S(1)}, u32[]{:S(2)}, u32[]{:S(2)}) collective-permute-start(f32[5,4,48,130]{3,2,1,0:T(8,128)S(1)} %get-tuple-element.38), channel_id=1, source_target_pairs={{8,0},{9,3},{10,6},{11,9},{12,12},{13,15},{24,16},{25,19},{26,22},... | collective-permute-start | bytes 1497608 | tf_op jit(solution)/shard_map/ppermute | solution.py:137
  57.6 52.2 %collective-permute-start.9 = (f32[5,4,48,130]{3,2,1,0:T(8,128)S(1)}, f32[5,4,48,130]{3,2,1,0:T(8,128)S(1)}, u32[]{:S(2)}, u32[]{:S(2)}) collective-permute-start(f32[5,4,48,130]{3,2,1,0:T(8,128)S(1)} %get-tuple-element.34), channel_id=1, source_target_pairs={{8,1},{9,4},{10,7},{11,10},{12,13},{24,17},{25,20},{26,23},{27,26}... | collective-permute-start | bytes 1497608 | tf_op jit(solution)/shard_map/ppermute | solution.py:137
  59.9 42.7 %copy-start.11 = (f32[5,4,1,384]{3,1,2,0:T(4,128)S(1)}, f32[5,4,1,384]{3,1,2,0:T(4,128)}, u32[]{:S(2)}) copy-start(f32[5,4,1,384]{3,1,2,0:T(4,128)} %copy.322) | copy-start | bytes 92164
  59.9 47.8 %copy-start.10 = (f32[5,4,1,384]{3,1,2,0:T(4,128)S(1)}, f32[5,4,1,384]{3,1,2,0:T(4,128)}, u32[]{:S(2)}) copy-start(f32[5,4,1,384]{3,1,2,0:T(4,128)} %copy.323) | copy-start | bytes 92164
  73.2 143.5 %collective-permute-start.2 = (f32[5,4,48,1]{3,2,1,0:T(8,128)}, f32[5,4,48,1]{3,2,1,0:T(8,128)}, u32[]{:S(2)}, u32[]{:S(2)}) collective-permute-start(f32[5,4,48,1]{3,2,1,0:T(8,128)} %get-tuple-element.30), channel_id=1, source_target_pairs={{0,1},{1,2},{2,3},{3,4},{4,5},{5,6},{6,7},{7,8},{8,9},{9,10},{10,1... | collective-permute-start | bytes 11528 | tf_op jit(solution)/shard_map/ppermute | solution.py:29
  81.9 134.7 %collective-permute-start.3 = (f32[5,4,48,1]{3,2,1,0:T(8,128)}, f32[5,4,48,1]{3,2,1,0:T(8,128)}, u32[]{:S(2)}, u32[]{:S(2)}) collective-permute-start(f32[5,4,48,1]{3,2,1,0:T(8,128)} %get-tuple-element.31), channel_id=1, source_target_pairs={{1,0},{2,1},{3,2},{4,3},{5,4},{6,5},{7,6},{8,7},{9,8},{10,9},{11,1... | collective-permute-start | bytes 11528 | tf_op jit(solution)/shard_map/ppermute | solution.py:30
  102.6 19.1 %collective-permute-start = (f32[5,4,1,384]{3,1,2,0:T(4,128)S(1)}, f32[5,4,1,384]{3,1,2,0:T(4,128)S(1)}, u32[]{:S(2)}, u32[]{:S(2)}) collective-permute-start(f32[5,4,1,384]{3,1,2,0:T(4,128)S(1)} %copy-done.11), channel_id=1, source_target_pairs={{0,16},{16,32},{32,48},{48,64},{64,80},{80,96},{96,112},{1,17},{17... | collective-permute-start | bytes 92168 | tf_op jit(solution)/shard_map/ppermute | solution.py:27
  107.7 14.7 %collective-permute-start.1 = (f32[5,4,1,384]{3,1,2,0:T(4,128)S(1)}, f32[5,4,1,384]{3,1,2,0:T(4,128)S(1)}, u32[]{:S(2)}, u32[]{:S(2)}) collective-permute-start(f32[5,4,1,384]{3,1,2,0:T(4,128)S(1)} %copy-done.10), channel_id=1, source_target_pairs={{16,0},{32,16},{48,32},{64,48},{80,64},{96,80},{112,96},{17,1},{33... | collective-permute-start | bytes 92168 | tf_op jit(solution)/shard_map/ppermute | solution.py:28
  221.3 14.6 %collective-permute-start.15 = (f32[5,4,48,1]{3,2,1,0:T(8,128)S(1)}, f32[5,4,48,1]{3,2,1,0:T(8,128)S(1)}, u32[]{:S(2)}, u32[]{:S(2)}) collective-permute-start(f32[5,4,48,1]{3,2,1,0:T(8,128)S(1)} %get-tuple-element.22), channel_id=1, source_target_pairs={{0,1},{1,2},{2,3},{3,4},{4,5},{5,6},{6,7},{7,8},{8,9},{9,10},{10,1... | collective-permute-start | bytes 11528 | tf_op jit(solution)/shard_map/ppermute | solution.py:29
  224.5 11.8 %collective-permute-start.16 = (f32[5,4,48,1]{3,2,1,0:T(8,128)S(1)}, f32[5,4,48,1]{3,2,1,0:T(8,128)S(1)}, u32[]{:S(2)}, u32[]{:S(2)}) collective-permute-start(f32[5,4,48,1]{3,2,1,0:T(8,128)S(1)} %get-tuple-element.23), channel_id=1, source_target_pairs={{1,0},{2,1},{3,2},{4,3},{5,4},{6,5},{7,6},{8,7},{9,8},{10,9},{11,1... | collective-permute-start | bytes 11528 | tf_op jit(solution)/shard_map/ppermute | solution.py:30
  226.7 7.0 %collective-permute-start.13 = (f32[5,4,1,384]{3,1,2,0:T(4,128)S(1)}, f32[5,4,1,384]{3,1,2,0:T(4,128)S(1)}, u32[]{:S(2)}, u32[]{:S(2)}) collective-permute-start(f32[5,4,1,384]{3,1,2,0:T(4,128)S(1)} %copy.310), channel_id=1, source_target_pairs={{0,16},{16,32},{32,48},{48,64},{64,80},{80,96},{96,112},{1,17},{17... | collective-permute-start | bytes 92168 | tf_op jit(solution)/shard_map/ppermute | solution.py:27
  230.3 5.6 %collective-permute-start.14 = (f32[5,4,1,384]{3,1,2,0:T(4,128)S(1)}, f32[5,4,1,384]{3,1,2,0:T(4,128)S(1)}, u32[]{:S(2)}, u32[]{:S(2)}) collective-permute-start(f32[5,4,1,384]{3,1,2,0:T(4,128)S(1)} %copy.312), channel_id=1, source_target_pairs={{16,0},{32,16},{48,32},{64,48},{80,64},{96,80},{112,96},{17,1},{33... | collective-permute-start | bytes 92168 | tf_op jit(solution)/shard_map/ppermute | solution.py:28
  238.6 16.6 %collective-permute-start.19 = (f32[5,4,48,1]{3,2,1,0:T(8,128)S(1)}, f32[5,4,48,1]{3,2,1,0:T(8,128)S(1)}, u32[]{:S(2)}, u32[]{:S(2)}) collective-permute-start(f32[5,4,48,1]{3,2,1,0:T(8,128)S(1)} %get-tuple-element.14), channel_id=1, source_target_pairs={{0,1},{1,2},{2,3},{3,4},{4,5},{5,6},{6,7},{7,8},{8,9},{9,10},{10,1... | collective-permute-start | bytes 11528 | tf_op jit(solution)/shard_map/ppermute | solution.py:29
  241.5 13.7 %collective-permute-start.20 = (f32[5,4,48,1]{3,2,1,0:T(8,128)S(1)}, f32[5,4,48,1]{3,2,1,0:T(8,128)S(1)}, u32[]{:S(2)}, u32[]{:S(2)}) collective-permute-start(f32[5,4,48,1]{3,2,1,0:T(8,128)S(1)} %get-tuple-element.15), channel_id=1, source_target_pairs={{1,0},{2,1},{3,2},{4,3},{5,4},{6,5},{7,6},{8,7},{9,8},{10,9},{11,1... | collective-permute-start | bytes 11528 | tf_op jit(solution)/shard_map/ppermute | solution.py:30
  244.6 7.7 %collective-permute-start.17 = (f32[5,4,1,384]{3,1,2,0:T(4,128)S(1)}, f32[5,4,1,384]{3,1,2,0:T(4,128)S(1)}, u32[]{:S(2)}, u32[]{:S(2)}) collective-permute-start(f32[5,4,1,384]{3,1,2,0:T(4,128)S(1)} %copy.315), channel_id=1, source_target_pairs={{0,16},{16,32},{32,48},{48,64},{64,80},{80,96},{96,112},{1,17},{17... | collective-permute-start | bytes 92168 | tf_op jit(solution)/shard_map/ppermute | solution.py:27
  249.6 5.5 %collective-permute-start.18 = (f32[5,4,1,384]{3,1,2,0:T(4,128)S(1)}, f32[5,4,1,384]{3,1,2,0:T(4,128)S(1)}, u32[]{:S(2)}, u32[]{:S(2)}) collective-permute-start(f32[5,4,1,384]{3,1,2,0:T(4,128)S(1)} %copy.317), channel_id=1, source_target_pairs={{16,0},{32,16},{48,32},{64,48},{80,64},{96,80},{112,96},{17,1},{33... | collective-permute-start | bytes 92168 | tf_op jit(solution)/shard_map/ppermute | solution.py:28
  341.3 28.9 %all-to-all-start = ((f32[8,5,4,16,128]{4,3,2,1,0:T(8,128)}), f32[8,5,4,16,128]{4,3,2,1,0:T(8,128)S(1)}, u32[]{:S(2)}, u32[]{:S(2)}) async-start(f32[8,5,4,16,128]{4,3,2,1,0:T(8,128)} %stack.79), calls=%async_computation | async-start | bytes 2621440 | tf_op jit(solution)/shard_map/all_to_all | solution.py:16
  370.4 46.9 %collective-permute-start.21 = (f32[5,4,48,128]{3,2,1,0:T(8,128)S(1)}, f32[5,4,48,128]{3,2,1,0:T(8,128)S(1)}, u32[]{:S(2)}, u32[]{:S(2)}) collective-permute-start(f32[5,4,48,128]{3,2,1,0:T(8,128)S(1)} %pad_dynamic-slice_fusion.13), channel_id=1, source_target_pairs={{1,9},{4,10},{7,11},{10,12},{13,13},{17,25},{20,26},{23,27},{26,28... | collective-permute-start | bytes 1474568 | tf_op jit(solution)/shard_map/ppermute | solution.py:169
  371.7 45.6 %collective-permute-start.22 = (f32[5,4,48,128]{3,2,1,0:T(8,128)S(1)}, f32[5,4,48,128]{3,2,1,0:T(8,128)S(1)}, u32[]{:S(2)}, u32[]{:S(2)}) collective-permute-start(f32[5,4,48,128]{3,2,1,0:T(8,128)S(1)} %pad_dynamic-slice_fusion.13), channel_id=1, source_target_pairs={{2,9},{5,10},{8,11},{11,12},{14,13},{18,25},{21,26},{24,27},{27,28... | collective-permute-start | bytes 1474568 | tf_op jit(solution)/shard_map/ppermute | solution.py:169
  373.7 43.8 %collective-permute-start.23 = (f32[5,4,48,128]{3,2,1,0:T(8,128)S(1)}, f32[5,4,48,128]{3,2,1,0:T(8,128)S(1)}, u32[]{:S(2)}, u32[]{:S(2)}) collective-permute-start(f32[5,4,48,128]{3,2,1,0:T(8,128)S(1)} %pad_dynamic-slice_fusion.13), channel_id=1, source_target_pairs={{0,8},{3,9},{6,10},{9,11},{12,12},{15,13},{16,24},{19,25},{22,26},... | collective-permute-start | bytes 1474568 | tf_op jit(solution)/shard_map/ppermute | solution.py:169
  380.2 37.3 %collective-permute-start.24 = (f32[5,4,48,128]{3,2,1,0:T(8,128)S(1)}, f32[5,4,48,128]{3,2,1,0:T(8,128)S(1)}, u32[]{:S(2)}, u32[]{:S(2)}) collective-permute-start(f32[5,4,48,128]{3,2,1,0:T(8,128)S(1)} %pad_dynamic-slice_fusion.13), channel_id=1, source_target_pairs={{1,8},{4,9},{7,10},{10,11},{13,12},{17,24},{20,25},{23,26},{26,27}... | collective-permute-start | bytes 1474568 | tf_op jit(solution)/shard_map/ppermute | solution.py:169
  381.6 47.5 %collective-permute-start.25 = (f32[5,4,48,128]{3,2,1,0:T(8,128)S(1)}, f32[5,4,48,128]{3,2,1,0:T(8,128)S(1)}, u32[]{:S(2)}, u32[]{:S(2)}) collective-permute-start(f32[5,4,48,128]{3,2,1,0:T(8,128)S(1)} %pad_dynamic-slice_fusion.13), channel_id=1, source_target_pairs={{2,8},{5,9},{8,10},{11,11},{14,12},{18,24},{21,25},{24,26},{27,27}... | collective-permute-start | bytes 1474568 | tf_op jit(solution)/shard_map/ppermute | solution.py:169
  417.4 11.7 %copy-start.3 = (f32[5,4,48,384]{3,2,1,0:T(8,128)S(1)}, f32[5,4,48,384]{3,2,1,0:T(8,128)}, u32[]{:S(2)}) copy-start(f32[5,4,48,384]{3,2,1,0:T(8,128)} %copy-done.2) | copy-start | bytes 4423684
  (10 other events, 42.5 us)
Sparse Core Ops, SparseCore 0:
  118.4 88.0 all-reduce.5
